TPU v7x, 512 devices: a whole 4x8x8 slice. The times are simulated.
512 devices in a mesh: group: 16 (over z, y_hi), rep: 32 (over x, y_lo, core).
Axes of the slice: x: 4, y: 8 (y_hi: 2, y_lo: 4; y = y_hi * 4 + y_lo), z: 8, core: 2. Of those that a mesh axis runs over, the one named last changes fastest.
Arguments:
- tokens: bfloat16 [16, 8192, 2048], P('group', 'rep'), may hold values from -6 to 6
- cotangent: bfloat16 [16, 8192, 4096], P('group', 'rep'), may hold values from -6 to 6
- gate_weight: float32 [16, 32, 256, 128], P('group', 'rep'), may hold values from -5 to 5
- up_weight: float32 [16, 32, 256, 128], P('group', 'rep'), may hold values from -5 to 5
- tile_rows: int32 [32, 2], replicated, may hold values from 0 to 15, as said below
- step: int32 [1], replicated, may hold values from 0 to 999
Outputs:
- new_gate: float32 [16, 32, 256, 128], P('group', 'rep')
Inputs may be any that keep to these rules, and one draw needn't show every extreme that they name: `tile_rows`: the 2 entries of a row are distinct, and every feature block is named by some row.
All inputs are finite; a program needn't handle non-finite values.
Results may differ from a plain program's by a relative error of at most 0.0024.
Values may be sent and summed in bfloat16 or wider, within the bound.
No kernel may reach another device: no remote copies, remote signals or barrier semaphores. Data moves between devices by JAX's collectives and lax.ppermute only.
A program may use at most 64 MiB of HBM per device.

v0:
```python
from functools import partial
import jax
import jax.numpy as jnp
from jax import lax
from jax.sharding import PartitionSpec as P

TILE = 128
PER_COL = 2
LEARNING_RATE = 0.1


def partner(value, axis, bit):
    return lax.ppermute(value, axis, [(i, i ^ 1 << bit) for i in range(lax.axis_size(axis))])


def trade(values, which_bit):
    return partner(values, "group", which_bit)


def body(tokens, cotangent, gate_weight, up_weight, tile_rows, step):
    scaling = (PER_COL * TILE) ** (-0.5)
    activations = tokens[0]
    cot_rows = cotangent[0]
    row_count = activations.shape[0]
    blocks = activations.shape[1] // TILE
    hidden = cot_rows.shape[1] // TILE
    one_hot = (tile_rows[:, :, None] == jnp.arange(blocks, dtype=jnp.int32)).astype(jnp.bfloat16)
    selected = jnp.einsum(
        "tdc,fkd->tfkc",
        activations.reshape(row_count, blocks, TILE),
        one_hot,
        preferred_element_type=jnp.float32,
    ).astype(jnp.bfloat16)
    selected = selected.reshape(row_count, hidden, PER_COL * TILE)
    master_gate = gate_weight[0]
    local_pair = jnp.concatenate([master_gate, up_weight[0]], -1).astype(jnp.bfloat16)
    combined = (
        jnp.einsum(
            "tfk,fke->tfe",
            selected,
            lax.all_gather(local_pair, "rep", axis=0, tiled=True),
            preferred_element_type=jnp.float32,
        )
        * scaling
    )
    gate_vals = combined[..., :TILE]
    up_vals = combined[..., TILE:]
    cot_blocks = cot_rows.reshape(row_count, hidden, TILE)
    sigmoid_gate = jax.nn.sigmoid(gate_vals)
    grad_gate = (
        cot_blocks * up_vals * sigmoid_gate * (1.0 + gate_vals * (1.0 - sigmoid_gate))
    ).astype(jnp.bfloat16)
    local_grad = (
        jnp.einsum("tfk,tfe->fke", selected, grad_gate, preferred_element_type=jnp.float32)
        * scaling
    )
    own_count = local_pair.shape[0]
    summed = lax.psum(local_grad, "rep")
    grad_share = lax.dynamic_slice_in_dim(summed, lax.axis_index("rep") * own_count, own_count, 0)
    stepped = master_gate - LEARNING_RATE * grad_share
    levels = lax.axis_size("group").bit_length() - 1
    chosen_bit = step[0] % levels
    branches = [partial(trade, which_bit=number) for number in range(levels)]
    partner_vals = lax.switch(chosen_bit, branches, stepped)
    averaged = 0.5 * (stepped + partner_vals)
    return averaged[None]


def solution(mesh):
    placed = (
        P("group", "rep", None),
        P("group", "rep", None),
        P("group", "rep", None, None),
        P("group", "rep", None, None),
        P(),
        P(),
    )
    return jax.shard_map(
        body, mesh=mesh, in_specs=placed, out_specs=P("group", "rep", None, None), check_vma=False
    )
```

profile of v0, /device:TPU:64, one launch (start us, length us, event | category | flops | bytes accessed | tf_op | source)
XLA Modules:
  0.0 406.5 jit_solution(12707755886064902224)
XLA Ops:
  6.5 0.0 all-gather.2.cloned.1.call-start
  6.5 1.0 bitcast_convert_fusion
  7.5 0.7 pad_maximum_fusion
  8.2 0.0 all-gather.2.cloned.1.call-update
  8.2 0.0 all-reduce.2.cloned.1.call-start
  8.3 1.5 copy.41
  9.7 3.9 convert_bitcast_fusion
  13.7 0.0 copy-start.2
  13.7 7.7 %copy.32 = bf16[256,32,2,128]{0,3,2,1:T(8,128)(2,1)} copy(bf16[256,32,2,128]{3,1,0,2:T(8,128)(2,1)} %convert_bitcast_fusion) | data formatting | bytes 8388608 | tf_op jit(solution)/shard_map/convert_element_type | solution.py:33
  21.4 0.0 copy-done.2
  21.4 3.0 copy.33
  24.4 54.1 %all-gather.2.cloned.1.call-done = bf16[32,256,256]{2,1,0:T(8,128)(2,1)} async-done(((bf16[1,256,256]{2,1,0:T(8,128)(2,1)}), bf16[32,256,256]{2,1,0:T(8,128)(2,1)}) %all-gather.2.cloned.1.call-update) | async-done | bytes 4194320 | tf_op jit(solution)/shard_map/all_gather | solution.py:41
  78.5 5.0 %multiply_bitcast_fusion = f32[256,32,256]{0,2,1:T(8,128)S(1)} fusion(bf16[32,256,256]{2,1,0:T(8,128)(2,1)} %all-gather.2.cloned.1.call-done, bf16[256,32,256]{0,2,1:T(8,128)(2,1)} %bitcast.31), kind=kOutput, calls=%fused_computation | convolution fusion | flops 1075838976 | bytes 16777216 | tf_op jit(solution)/shard_map/tfk,fke->tfe/dot_general | solution.py:38
  83.4 0.0 copy-done
  83.4 0.9 copy-done.1
  84.4 3.8 convolution_multiply_fusion
  88.1 0.0 all-reduce.2.cloned.1.call-update
  88.9 297.4 %all-reduce.2.cloned.1.call-done = f32[32,256,128]{2,1,0:T(8,128)} async-done(((f32[32,256,128]{2,1,0:T(8,128)}), f32[32,256,128]{2,1,0:T(8,128)}) %all-reduce.2.cloned.1.call-update) | async-done | bytes 4194320 | tf_op jit(solution)/shard_map/psum | solution.py:58
  386.3 0.0 copy-done.3
  386.3 0.9 bitcast_subtract_fusion
  387.2 10.9 %conditional.1 = (f32[1,256,128]{2,1,0:T(8,128)}) conditional(s32[]{:T(128)} %clamp.3, f32[1,256,128]{2,1,0:T(8,128)S(1)} %bitcast_subtract_fusion, f32[1,256,128]{2,1,0:T(8,128)S(1)} %bitcast_subtract_fusion, f32[1,256,128]{2,1,0:T(8,128)S(1)} %bitcast_subtract_fusion, ...), branch_computations={%region_1.2_spmd, %region_2.3_spmd, %region_3.4_spmd, %region_4.5_... | conditional | bytes 524336 | solution.py:64
  387.2 6.0 %collective-permute-start = (f32[1,256,128]{2,1,0:T(8,128)S(1)}, f32[1,256,128]{2,1,0:T(8,128)}, u32[]{:S(2)}, u32[]{:S(2)}) collective-permute-start(f32[1,256,128]{2,1,0:T(8,128)S(1)} %param), channel_id=1, source_target_pairs={{0,32},{32,0},{64,96},{96,64},{128,160},{160,128},{192,224},{224,1... | collective-permute-start | bytes 393224 | tf_op jit(solution)/shard_map/cond/branch_0_fun/ppermute | solution.py:13
  393.3 4.8 %collective-permute-done = f32[1,256,128]{2,1,0:T(8,128)} collective-permute-done((f32[1,256,128]{2,1,0:T(8,128)S(1)}, f32[1,256,128]{2,1,0:T(8,128)}, u32[]{:S(2)}, u32[]{:S(2)}) %collective-permute-start) | collective-permute-done | bytes 131104 | tf_op jit(solution)/shard_map/cond/branch_0_fun/ppermute | solution.py:13
  398.1 1.6 multiply_bitcast_fusion.1
  (3 shorter events, 0.0 us)
Async XLA Ops:
  6.5 71.9 %all-gather.2.cloned.1.call-start = ((), (), s32[]{:S(2)}) async-start(), calls=%async_computation | async-start | bytes 4325376 | tf_op jit(solution)/shard_map/all_gather | solution.py:41
  8.2 378.0 %all-reduce.2.cloned.1.call-start = ((), (), s32[]{:S(2)}) async-start(), calls=%async_computation.1 | async-start | bytes 8388608 | tf_op jit(solution)/shard_map/psum | solution.py:58
  13.7 7.7 %copy-start.2 = (bf16[1,256,4096]{2,1,0:T(8,128)(2,1)S(1)}, bf16[1,256,4096]{2,1,0:T(8,128)(2,1)}, u32[]{:S(2)}) copy-start(bf16[1,256,4096]{2,1,0:T(8,128)(2,1)} %param.11) | copy-start | bytes 6291460
  78.5 5.0 %copy-start = (bf16[256,32,2,128]{0,3,2,1:T(8,128)(2,1)S(1)}, bf16[256,32,2,128]{0,3,2,1:T(8,128)(2,1)}, u32[]{:S(2)}) copy-start(bf16[256,32,2,128]{0,3,2,1:T(8,128)(2,1)} %copy.32) | copy-start | bytes 12582916
  78.5 5.9 %copy-start.1 = (f32[1,256,4096]{1,2,0:T(8,128)S(1)}, f32[1,256,4096]{1,2,0:T(8,128)}, u32[]{:S(2)}) copy-start(f32[1,256,4096]{1,2,0:T(8,128)} %copy.33) | copy-start | bytes 12582916
  88.1 298.1 %copy-start.3 = (f32[1,1,256,128]{3,2,1,0:T(8,128)S(1)}, f32[1,1,256,128]{3,2,1,0:T(8,128)}, u32[]{:S(2)}) copy-start(f32[1,1,256,128]{3,2,1,0:T(8,128)} %param.12) | copy-start | bytes 393220
  387.2 10.9 %collective-permute-start = (f32[1,256,128]{2,1,0:T(8,128)S(1)}, f32[1,256,128]{2,1,0:T(8,128)}, u32[]{:S(2)}, u32[]{:S(2)}) collective-permute-start(f32[1,256,128]{2,1,0:T(8,128)S(1)} %param), channel_id=1, source_target_pairs={{0,32},{32,0},{64,96},{96,64},{128,160},{160,128},{192,224},{224,1... | collective-permute-start | bytes 393224 | tf_op jit(solution)/shard_map/cond/branch_0_fun/ppermute | solution.py:13
Sparse Core Ops, SparseCore 0:
  9.5 68.9 all-gather.1
  88.3 297.9 all-reduce.1
where the time goes:
time: 407 us; the launch traced here: 406 us
  waiting for transfers between devices  356 us (87%)
  between operations  14.1 us (3%)
  local copies, waits for them, and re-layouts  13.1 us (3%)
  matrix products  12.6 us (3%)
  starting transfers between devices  6.09 us (1%)
  other arithmetic  4.15 us (1%)
    psum x1, waiting for transfers between devices, body(): summed = lax.psum(local_grad, 'rep')  297 us
    all_gather x1, waiting for transfers between devices, body(): lax.all_gather(local_pair, 'rep', axis=0, tiled=True)  54.1 us
  transfers between devices with their start and end apart: 3, of which 3 were waited for; matrix products, arithmetic and copies ran while one was open for 4% of the time, Pallas kernels for 0%

commit v1 on v0

--- a/solution.py
+++ b/solution.py
@@ -38,7 +38,9 @@
         jnp.einsum(
             "tfk,fke->tfe",
             selected,
-            lax.all_gather(local_pair, "rep", axis=0, tiled=True),
+            jnp.concatenate(
+                lax.all_to_all(jnp.stack([local_pair] * lax.axis_size("rep")), "rep", 0, 0), axis=0
+            ),
             preferred_element_type=jnp.float32,
         )
         * scaling

time: 407 us -> 443 us (1.088)
  waiting for transfers between devices: 356 us -> 384 us
  starting transfers between devices: 6.09 us -> 14.3 us
    all_to_all x0 -> x1, waiting for transfers between devices: none -> 81.1 us  [body(): lax.all_to_all(jnp.stack([local_pair] * lax.axis_size('rep')), 'rep', 0, 0)]
    all_gather x1 -> x0, waiting for transfers between devices: 54.1 us -> none  [body(): lax.all_gather(local_pair, 'rep', axis=0, tiled=True)]
    all_to_all x0 -> x1, starting transfers between devices: none -> 7.99 us  [body(): lax.all_to_all(jnp.stack([local_pair] * lax.axis_size('rep')), 'rep', 0, 0)]
  transfers between devices with their start and end apart: 3 -> 3, of which waited for: 3 -> 3; matrix products, arithmetic and copies ran while one was open for 4% -> 3% of each run, Pallas kernels for 0% -> 0%
where the time goes in v1:
time: 443 us; the launch traced here: 442 us
  waiting for transfers between devices  384 us (87%)
  local copies, waits for them, and re-layouts  14.4 us (3%)
  starting transfers between devices  14.3 us (3%)
  between operations  14.2 us (3%)
  matrix products  11.8 us (3%)
    psum x1, waiting for transfers between devices, body(): summed = lax.psum(local_grad, 'rep')  298 us
    all_to_all x1, waiting for transfers between devices, body(): lax.all_to_all(jnp.stack([local_pair] * lax.axis_size('rep')), 'rep', 0, 0)  81.1 us
  transfers between devices with their start and end apart: 3, of which 3 were waited for; matrix products, arithmetic and copies ran while one was open for 3% of the time, Pallas kernels for 0%

profile of v1, /device:TPU:64, one launch (start us, length us, event | category | flops | bytes accessed | tf_op | source)
XLA Modules:
  0.0 442.4 jit_solution(14161403738695014632)
XLA Ops:
  6.5 1.0 convert_bitcast_fusion.1
  7.5 0.1 copy.18
  7.7 2.4 stack.2
  10.1 8.0 %all-to-all-start = ((bf16[32,1,256,256]{2,3,1,0:T(8,128)(2,1)}), bf16[32,1,256,256]{2,3,1,0:T(8,128)(2,1)}, u32[]{:S(2)}, u32[]{:S(2)}) async-start(bf16[32,1,256,256]{2,3,1,0:T(8,128)(2,1)} %stack.2), calls=%async_computation | async-start | bytes 8388608 | tf_op jit(solution)/shard_map/all_to_all | solution.py:42
  18.1 0.0 all-reduce.2.cloned.1.call-start
  18.1 0.0 copy-done.3
  18.2 0.2 copy.24
  18.4 0.0 copy-done.5
  18.4 3.2 convert_bitcast_fusion
  21.6 7.7 %copy.16 = bf16[256,32,2,128]{0,3,2,1:T(8,128)(2,1)} copy(bf16[256,32,2,128]{3,1,0,2:T(8,128)(2,1)} %convert_bitcast_fusion) | data formatting | bytes 8388608 | tf_op jit(solution)/shard_map/convert_element_type | solution.py:33
  29.3 0.0 copy-done.2
  29.3 2.9 copy.17
  32.2 81.1 %all-to-all-done = bf16[32,1,256,256]{2,3,1,0:T(8,128)(2,1)} async-done(((bf16[32,1,256,256]{2,3,1,0:T(8,128)(2,1)}), bf16[32,1,256,256]{2,3,1,0:T(8,128)(2,1)}, u32[]{:S(2)}, u32[]{:S(2)}) %all-to-all-start) | async-done | bytes 4194336 | tf_op jit(solution)/shard_map/all_to_all | solution.py:42
  113.4 4.9 %multiply_bitcast_fusion = f32[256,32,256]{0,2,1:T(8,128)S(1)} fusion(bf16[256,32,256]{0,2,1:T(8,128)(2,1)} %bitcast.36, bf16[32,1,256,256]{2,3,1,0:T(8,128)(2,1)} %all-to-all-done), kind=kOutput, calls=%fused_computation | convolution fusion | flops 1075838976 | bytes 16777216 | tf_op jit(solution)/shard_map/tfk,fke->tfe/dot_general | solution.py:38
  118.2 0.0 copy-done
  118.2 1.0 copy-done.1
  119.3 3.8 convolution_multiply_fusion
  123.1 0.0 all-reduce.2.cloned.1.call-update
  123.8 298.2 %all-reduce.2.cloned.1.call-done = f32[32,256,128]{2,1,0:T(8,128)} async-done(((f32[32,256,128]{2,1,0:T(8,128)}), f32[32,256,128]{2,1,0:T(8,128)}) %all-reduce.2.cloned.1.call-update) | async-done | bytes 4194320 | tf_op jit(solution)/shard_map/psum | solution.py:60
  422.0 0.9 bitcast_subtract_fusion
  422.9 11.0 %conditional.1 = (f32[1,256,128]{2,1,0:T(8,128)}) conditional(s32[]{:T(128)} %clamp.3, f32[1,256,128]{2,1,0:T(8,128)S(1)} %bitcast_subtract_fusion, f32[1,256,128]{2,1,0:T(8,128)S(1)} %bitcast_subtract_fusion, f32[1,256,128]{2,1,0:T(8,128)S(1)} %bitcast_subtract_fusion, ...), branch_computations={%region_1.2_spmd, %region_2.3_spmd, %region_3.4_spmd, %region_4.5_... | conditional | bytes 524336 | solution.py:66
  422.9 6.3 %collective-permute-start = (f32[1,256,128]{2,1,0:T(8,128)S(1)}, f32[1,256,128]{2,1,0:T(8,128)}, u32[]{:S(2)}, u32[]{:S(2)}) collective-permute-start(f32[1,256,128]{2,1,0:T(8,128)S(1)} %param), channel_id=1, source_target_pairs={{0,32},{32,0},{64,96},{96,64},{128,160},{160,128},{192,224},{224,1... | collective-permute-start | bytes 393224 | tf_op jit(solution)/shard_map/cond/branch_0_fun/ppermute | solution.py:13
  429.2 4.7 %collective-permute-done = f32[1,256,128]{2,1,0:T(8,128)} collective-permute-done((f32[1,256,128]{2,1,0:T(8,128)S(1)}, f32[1,256,128]{2,1,0:T(8,128)}, u32[]{:S(2)}, u32[]{:S(2)}) %collective-permute-start) | collective-permute-done | bytes 131104 | tf_op jit(solution)/shard_map/cond/branch_0_fun/ppermute | solution.py:13
  434.0 1.6 multiply_bitcast_fusion.1
  (8 shorter events, 0.0 us)
Async XLA Ops:
  10.1 8.1 %copy-start.3 = (bf16[1,256,2048]{2,1,0:T(8,128)(2,1)S(1)}, bf16[1,256,2048]{2,1,0:T(8,128)(2,1)}, u32[]{:S(2)}) copy-start(bf16[1,256,2048]{2,1,0:T(8,128)(2,1)} %param.10) | copy-start | bytes 3145732
  10.1 8.3 %copy-start.5 = (s32[32,2]{0,1:T(2,128)S(1)}, s32[32,2]{0,1:T(2,128)}, u32[]{:S(2)}) copy-start(s32[32,2]{0,1:T(2,128)} %param.14) | copy-start | bytes 772
  10.1 103.3 %all-to-all-start = ((bf16[32,1,256,256]{2,3,1,0:T(8,128)(2,1)}), bf16[32,1,256,256]{2,3,1,0:T(8,128)(2,1)}, u32[]{:S(2)}, u32[]{:S(2)}) async-start(bf16[32,1,256,256]{2,3,1,0:T(8,128)(2,1)} %stack.2), calls=%async_computation | async-start | bytes 8388608 | tf_op jit(solution)/shard_map/all_to_all | solution.py:42
  18.1 403.9 %all-reduce.2.cloned.1.call-start = ((), (), s32[]{:S(2)}) async-start(), calls=%async_computation.1 | async-start | bytes 8388608 | tf_op jit(solution)/shard_map/psum | solution.py:60
  21.6 7.7 %copy-start.2 = (bf16[1,256,4096]{2,1,0:T(8,128)(2,1)S(1)}, bf16[1,256,4096]{2,1,0:T(8,128)(2,1)}, u32[]{:S(2)}) copy-start(bf16[1,256,4096]{2,1,0:T(8,128)(2,1)} %param.11) | copy-start | bytes 6291460
  113.4 4.9 %copy-start = (bf16[256,32,2,128]{0,3,2,1:T(8,128)(2,1)S(1)}, bf16[256,32,2,128]{0,3,2,1:T(8,128)(2,1)}, u32[]{:S(2)}) copy-start(bf16[256,32,2,128]{0,3,2,1:T(8,128)(2,1)} %copy.16) | copy-start | bytes 12582916
  113.4 5.9 %copy-start.1 = (f32[1,256,4096]{1,2,0:T(8,128)S(1)}, f32[1,256,4096]{1,2,0:T(8,128)}, u32[]{:S(2)}) copy-start(f32[1,256,4096]{1,2,0:T(8,128)} %copy.17) | copy-start | bytes 12582916
  123.1 299.0 %copy-start.4 = (f32[1,1,256,128]{3,2,1,0:T(8,128)S(1)}, f32[1,1,256,128]{3,2,1,0:T(8,128)}, u32[]{:S(2)}) copy-start(f32[1,1,256,128]{3,2,1,0:T(8,128)} %param.12) | copy-start | bytes 393220
  422.9 11.0 %collective-permute-start = (f32[1,256,128]{2,1,0:T(8,128)S(1)}, f32[1,256,128]{2,1,0:T(8,128)}, u32[]{:S(2)}, u32[]{:S(2)}) collective-permute-start(f32[1,256,128]{2,1,0:T(8,128)S(1)} %param), channel_id=1, source_target_pairs={{0,32},{32,0},{64,96},{96,64},{128,160},{160,128},{192,224},{224,1... | collective-permute-start | bytes 393224 | tf_op jit(solution)/shard_map/cond/branch_0_fun/ppermute | solution.py:13
Sparse Core Ops, SparseCore 0:
  123.2 298.7 all-reduce.1
